TPU v7x, 256 devices: a whole 4x4x8 slice. The times are simulated.
256 devices in a mesh: dp: 16 (over z, core), expert: 16 (over y, x).
Axes of the slice: x: 4, y: 4, z: 8, core: 2. Of those that a mesh axis runs over, the one named last changes fastest.
Arguments:
- cotangent: bfloat16 [32768, 2048], P(('dp', 'expert')), may hold values from -6 to 6
- saved_gate_up: bfloat16 [32768, 8, 1536], P(('dp', 'expert')), may hold values from -6 to 6
- route_ids: int32 [32768, 8], P(('dp', 'expert')), may hold values from 0 to 31, all different within a row; in each aligned block of 128 rows (0 to 127, 128 to 255, ...) at most 64 rows name the same one
- route_weights: float32 [32768, 8], P(('dp', 'expert')), may hold values from 0.05 to 1
- w_down: bfloat16 [32, 768, 2048], P('expert', 'dp'), may hold values from -0.21875 to 0.21875
Outputs:
- grad_gate_up: bfloat16 [32768, 8, 1536], P(('dp', 'expert'))
- route_grad: float32 [32768, 8], P(('dp', 'expert'))
- grad_down: float32 [32, 768, 2048], P('expert', 'dp')
Inputs may be any that keep to these rules, and one draw needn't show every extreme that they name: `route_ids`: within the rows of one device (aligned blocks of 128 tokens), no expert is named by more than 64 routes, and in every draw some expert is named by exactly 64; the 8 experts of a token are distinct.
All inputs are finite; a program needn't handle non-finite values.
Results may differ from a plain program's by a relative error of at most 0.02.
Values may be sent and summed in bfloat16 or wider, within the bound.
A program may use at most 128 MiB of HBM per device.

v0:
```python
import jax
import jax.numpy as jnp
from jax import lax
from jax.sharding import PartitionSpec as P


def slot_counts(ids, experts):
    routes = ids.shape[-1]
    onehot = (ids[..., None] == jnp.arange(experts, dtype=jnp.int32)).astype(jnp.bfloat16)
    lower = (jnp.arange(routes)[:, None] > jnp.arange(routes)[None, :]).astype(jnp.bfloat16)
    before = jnp.einsum("rq,...qe->...re", lower, onehot, preferred_element_type=jnp.float32)
    return jnp.sum(before * onehot.astype(jnp.float32), axis=-1).astype(jnp.int32)


def local(cotangent, saved_gate_up, route_ids, route_weights, w_down):
    tokens, top = route_ids.shape
    width = cotangent.shape[1]
    hidden_units = saved_gate_up.shape[2] // 2
    owners = lax.axis_size("expert")
    replicas = lax.axis_size("dp")
    me = lax.axis_index("expert")
    local_experts = w_down.shape[0]
    experts = local_experts * owners
    capacity = min(tokens, 2 * tokens * top // experts)
    routes = tokens * top
    cot_group = lax.all_gather(cotangent, "expert", axis=0, tiled=True)
    ids_group = lax.all_gather(route_ids.reshape(1, routes), "expert", axis=0, tiled=True)
    full_down = lax.all_gather(w_down, "dp", axis=1, tiled=True)
    gate = saved_gate_up[:, :, :hidden_units].astype(jnp.float32)
    up = saved_gate_up[:, :, hidden_units:].astype(jnp.float32)
    sig = jax.nn.sigmoid(gate)
    act = gate * sig
    hidden = (act * up).astype(jnp.bfloat16)
    weights = route_weights[:, :, None]
    scaled = (weights * hidden.astype(jnp.float32)).astype(jnp.bfloat16)
    flat_ids = route_ids.reshape(routes)
    slot = slot_counts(flat_ids, experts)
    position = flat_ids * capacity + slot
    slot_ids = jnp.arange(experts * capacity, dtype=jnp.int32)
    match = position[None, :] == slot_ids[:, None]
    route_of_slot = jnp.sum(
        jnp.where(match, jnp.arange(routes, dtype=jnp.int32)[None, :], 0), axis=1
    )
    filled = jnp.any(match, axis=1)
    h_rows = jnp.where(
        filled[:, None],
        scaled.reshape(routes, hidden_units)[route_of_slot],
        jnp.zeros((), jnp.bfloat16),
    )
    h_send = h_rows.reshape(owners, local_experts, capacity, hidden_units)
    slot_all = slot_counts(ids_group, experts)
    mine = me * local_experts + jnp.arange(local_experts, dtype=jnp.int32)
    pos_all = ids_group * capacity + slot_all
    want = (mine[:, None] * capacity + jnp.arange(capacity, dtype=jnp.int32)[None, :]).reshape(-1)
    hit = pos_all[:, None, :] == want[None, :, None]
    token_of = jnp.sum(
        jnp.where(hit, (jnp.arange(routes, dtype=jnp.int32) // top)[None, None, :], 0), axis=2
    )
    rows = (jnp.arange(owners, dtype=jnp.int32)[:, None] * tokens + token_of).reshape(
        owners, local_experts, capacity
    )
    rows = jnp.transpose(rows, (1, 0, 2)).reshape(local_experts, owners * capacity)
    dy_recv = cot_group[rows]
    h_recv = lax.all_to_all(h_send, "expert", split_axis=0, concat_axis=2, tiled=True)[0]
    grads = jnp.einsum(
        "jsd,jfd->jsf", dy_recv, full_down, preferred_element_type=jnp.float32
    ).astype(jnp.bfloat16)
    back = lax.all_to_all(
        grads.reshape(1, local_experts, owners * capacity, hidden_units),
        "expert",
        split_axis=2,
        concat_axis=0,
        tiled=True,
    )
    parts = []
    for j in range(local_experts):
        part = jnp.einsum(
            "sf,sd->fd", h_recv[j], dy_recv[j], preferred_element_type=jnp.float32
        ).astype(jnp.bfloat16)
        parts.append(
            lax.psum_scatter(part, "dp", scatter_dimension=0, tiled=True).astype(jnp.float32)
        )
    grad_down = jnp.stack(parts)
    returned_rows = back.reshape(experts * capacity, hidden_units)[position]
    qf = returned_rows.reshape(tokens, top, hidden_units).astype(jnp.float32)
    route_grad = jnp.sum(qf * hidden.astype(jnp.float32), -1)
    d_hidden = weights * qf
    d_gate = d_hidden * up * sig * (1.0 + gate * (1.0 - sig))
    d_up = d_hidden * act
    grad_gate_up = jnp.concatenate([d_gate, d_up], -1).astype(jnp.bfloat16)
    return (grad_gate_up, route_grad, grad_down)


def solution(mesh):
    return jax.shard_map(
        local,
        mesh=mesh,
        in_specs=(
            P(("dp", "expert"), None),
            P(("dp", "expert"), None, None),
            P(("dp", "expert"), None),
            P(("dp", "expert"), None),
            P("expert", "dp", None),
        ),
        out_specs=(
            P(("dp", "expert"), None, None),
            P(("dp", "expert"), None),
            P("expert", "dp", None),
        ),
        check_vma=False,
    )
```

profile of v0, /device:TPU:2, one launch (start us, length us, event | category | flops | bytes accessed | tf_op | source)
XLA Modules:
  0.0 409.4 jit_solution(11496074652841021074)
XLA Ops:
  7.2 0.0 all-gather.4.cloned.1.call-start
  7.2 0.7 all-gather.4.cloned.1.call-update
  7.9 0.0 all-gather.6.cloned.1.call-start
  7.9 0.7 all-gather.6.cloned.1.call-update
  8.7 0.8 copy.30
  9.4 0.1 reshape.205
  9.5 23.6 %all-gather = s32[16,1,1024]{2,1,0:T(1,128)S(1)} all-gather(s32[1,1,1024]{2,1,0:T(1,128)S(1)} %reshape.205), channel_id=1, replica_groups=mesh['dp'=16,'expert'=16] {'expert'}, dimensions={0}, use_global_device_ids=true | all-gather | bytes 69632 | tf_op jit(solution)/shard_map/all_gather | solution.py:27
  33.2 0.1 iota_add_fusion
  33.3 0.1 add.119
  33.4 1.4 fusion.27
  34.8 1.0 select_reduce_fusion.1
  35.8 0.1 reduce_sum.51
  35.9 0.1 add_bitcast_fusion
  36.0 0.1 reshape.171
  36.1 53.2 %all-gather.4.cloned.1.call-done = bf16[2048,2048]{1,0:T(8,128)(2,1)} async-done(((bf16[128,2048]{1,0:T(8,128)(2,1)}), bf16[2048,2048]{1,0:T(8,128)(2,1)}) %all-gather.4.cloned.1.call-update) | async-done | bytes 8388624 | tf_op jit(solution)/shard_map/all_gather | solution.py:26
  89.3 20.8 %gather_fusion = bf16[2048,2048]{1,0:T(8,128)(2,1)} fusion(bf16[2048,2048]{1,0:T(8,128)(2,1)} %all-gather.4.cloned.1.call-done, s32[2048]{0:T(1024)S(1)} %bitcast_clamp_fusion), kind=kCustom, calls=%fused_computation | custom fusion | bytes 16785408 | tf_op jit(solution)/shard_map/gather | solution.py:63
  110.1 26.9 %all-gather.6.cloned.1.call-done = bf16[2,768,2048]{2,1,0:T(8,128)(2,1)} async-done(((bf16[2,48,2048]{2,1,0:T(8,128)(2,1)}), bf16[2,768,2048]{2,1,0:T(8,128)(2,1)}) %all-gather.6.cloned.1.call-update) | async-done | bytes 6291472 | tf_op jit(solution)/shard_map/all_gather | solution.py:28
  136.9 11.0 %convert_bitcast_fusion = bf16[1,2,1024,768]{3,2,1,0:T(8,128)(2,1)S(1)} fusion(bf16[2,1024,2048]{2,1,0:T(8,128)(2,1)} %bitcast.55, bf16[2,768,2048]{2,1,0:T(8,128)(2,1)} %all-gather.6.cloned.1.call-done), kind=kOutput, calls=%fused_computation.38 | convolution fusion | flops 6444023808 | bytes 17825792 | tf_op jit(solution)/shard_map/jsd,jfd->jsf/dot_general | solution.py:65
  147.9 4.9 %copy.32 = bf16[1,2,1024,768]{3,1,0,2:T(2,128)(2,1)} copy(bf16[1,2,1024,768]{3,2,1,0:T(8,128)(2,1)S(1)} %convert_bitcast_fusion) | data formatting | bytes 6291456 | tf_op jit(solution)/shard_map/reshape | solution.py:69
  152.8 7.4 %all-to-all-start = ((bf16[1,2,1024,768]{3,1,0,2:T(2,128)(2,1)}), bf16[1,2,1024,768]{3,1,0,2:T(2,128)(2,1)S(1)}, u32[]{:S(2)}, u32[]{:S(2)}) async-start(bf16[1,2,1024,768]{3,1,0,2:T(2,128)(2,1)} %copy.32), calls=%async_computation | async-start | bytes 6291456 | tf_op jit(solution)/shard_map/all_to_all | solution.py:68
  160.2 0.0 reduce-scatter.5.cloned.1.call-start
  160.3 0.1 eq.60
  160.4 0.1 copy.29
  160.5 0.1 copy.34
  160.6 0.1 mul.102
  160.7 0.5 fusion.31
  161.3 1.0 fusion
  162.3 0.1 broadcast_in_dim.36
  162.4 0.9 select_reduce_fusion
  163.4 41.3 %all-to-all-done = bf16[1,2,1024,768]{3,1,0,2:T(2,128)(2,1)S(1)} async-done(((bf16[1,2,1024,768]{3,1,0,2:T(2,128)(2,1)}), bf16[1,2,1024,768]{3,1,0,2:T(2,128)(2,1)S(1)}, u32[]{:S(2)}, u32[]{:S(2)}) %all-to-all-start) | async-done | bytes 3145760 | tf_op jit(solution)/shard_map/all_to_all | solution.py:68
  204.7 1.7 copy-done.1
  206.3 2.5 copy.33
  208.9 5.2 %gather_fusion.1 = bf16[1024,768]{1,0:T(8,128)(2,1)} fusion(bf16[2048,768]{1,0:T(8,128)(2,1)S(1)} %bitcast.51, s32[1024]{0:T(1024)S(1)} %broadcast_clamp_fusion.1), kind=kCustom, calls=%fused_computation.1 | custom fusion | bytes 3149824 | tf_op jit(solution)/shard_map/gather | solution.py:84
  214.1 5.0 %fusion.29 = (bf16[1024,768]{1,0:T(8,128)(2,1)S(1)}, bf16[128,8,768]{2,1,0:T(8,128)(2,1)S(1)}, bf16[128,8,768]{2,1,0:T(8,128)(2,1)}, bf16[128,8,768]{2,1,0:T(8,128)(2,1)}) fusion(f32[128,8]{1,0:T(8,128)S(1)} %copy.29, bf16[128,8,1536]{2,1,0:T(8,128)(2,1)} %param.6, bf16[1024,768]{1,0:T(8,128)(2,1)} %gather_fusion.1), kind=kLoop, calls=%fused_computation.44 | loop fusion | flops 17301504 | bytes 11014144 | tf_op jit(solution)/shard_map/reshape | solution.py:47
  219.0 9.4 %gather_fusion.2 = bf16[2048,768]{1,0:T(8,128)(2,1)} fusion(bf16[1024,768]{1,0:T(8,128)(2,1)S(1)} %get-tuple-element.9, s32[2048]{0:T(1024)S(1)} %broadcast_clamp_fusion), kind=kCustom, calls=%fused_computation.2 | custom fusion | bytes 6299648 | tf_op jit(solution)/shard_map/gather | solution.py:47
  228.4 2.3 broadcast_select_fusion
  230.7 46.5 %all_to_all.30 = bf16[16,2,64,768]{3,2,1,0:T(8,128)(2,1)S(1)} all-to-all(bf16[16,2,64,768]{3,2,1,0:T(8,128)(2,1)S(1)} %broadcast_select_fusion), channel_id=1, replica_groups=mesh['dp'=16,'expert'=16] {'expert'}, dimensions={0} | all-to-all | bytes 6291456 | tf_op jit(solution)/shard_map/all_to_all | solution.py:64
  277.2 0.2 fusion.42
  277.5 4.9 %fusion.13 = bf16[768,2048]{1,0:T(8,128)(2,1)} fusion(bf16[1024,768]{1,0:T(8,128)(2,1)S(1)} %bitcast.59, bf16[2048,2048]{1,0:T(8,128)(2,1)S(1)} %bitcast.57), kind=kOutput, calls=%fused_computation.25 | convolution fusion | flops 3222798336 | bytes 8912896 | tf_op jit(solution)/shard_map/sf,sd->fd/dot_general | solution.py:77
  282.4 0.0 reduce-scatter.3.cloned.1.call-start
  282.5 7.0 %fusion.10 = bf16[768,2048]{1,0:T(8,128)(2,1)} fusion(bf16[1024,768]{1,0:T(8,128)(2,1)S(1)} %bitcast.58, bf16[2048,2048]{1,0:T(8,128)(2,1)} %gather_fusion), kind=kOutput, calls=%fused_computation.24 | convolution fusion | flops 3222798336 | bytes 8912896 | tf_op jit(solution)/shard_map/sf,sd->fd/dot_general | solution.py:77
  289.6 1.4 copy-done
  290.9 0.5 fusion.22
  291.4 0.7 copy.36
  292.1 3.8 pad_maximum_fusion
  295.9 43.3 %reduce-scatter.5.cloned.1.call-done = bf16[48,2048]{1,0:T(8,128)(2,1)} async-done(((bf16[768,2048]{1,0:T(8,128)(2,1)}), bf16[48,2048]{1,0:T(8,128)(2,1)}) %reduce-scatter.5.cloned.1.call-update) | async-done | bytes 196624 | tf_op jit(solution)/shard_map/reduce_scatter | solution.py:81
  339.2 61.7 %reduce-scatter.3.cloned.1.call-done = bf16[48,2048]{1,0:T(8,128)(2,1)} async-done(((bf16[768,2048]{1,0:T(8,128)(2,1)}), bf16[48,2048]{1,0:T(8,128)(2,1)}) %reduce-scatter.3.cloned.1.call-update) | async-done | bytes 196624 | tf_op jit(solution)/shard_map/reduce_scatter | solution.py:81
  400.9 2.0 maximum_convert_fusion
  (28 shorter events, 0.2 us)
Async XLA Ops:
  7.2 82.1 %all-gather.4.cloned.1.call-start = ((), (), s32[]{:S(2)}) async-start(), calls=%async_computation.4 | async-start | bytes 8912896 | tf_op jit(solution)/shard_map/all_gather | solution.py:26
  7.9 129.0 %all-gather.6.cloned.1.call-start = ((), (), s32[]{:S(2)}) async-start(), calls=%async_computation.5 | async-start | bytes 6684672 | tf_op jit(solution)/shard_map/all_gather | solution.py:28
  152.8 7.5 %copy-start.3 = (f32[128,8]{0,1:T(8,128)S(1)}, f32[128,8]{0,1:T(8,128)}, u32[]{:S(2)}) copy-start(f32[128,8]{0,1:T(8,128)} %param.8) | copy-start | bytes 12292
  152.8 7.7 %copy-start.2 = (s32[128,8]{0,1:T(8,128)S(1)}, s32[128,8]{0,1:T(8,128)}, u32[]{:S(2)}) copy-start(s32[128,8]{0,1:T(8,128)} %param.7) | copy-start | bytes 12292
  152.8 51.8 %all-to-all-start = ((bf16[1,2,1024,768]{3,1,0,2:T(2,128)(2,1)}), bf16[1,2,1024,768]{3,1,0,2:T(2,128)(2,1)S(1)}, u32[]{:S(2)}, u32[]{:S(2)}) async-start(bf16[1,2,1024,768]{3,1,0,2:T(2,128)(2,1)} %copy.32), calls=%async_computation | async-start | bytes 6291456 | tf_op jit(solution)/shard_map/all_to_all | solution.py:68
  160.2 179.0 %reduce-scatter.5.cloned.1.call-start = ((), (), s32[]{:S(2)}) async-start(), calls=%async_computation.7 | async-start | bytes 3342336 | tf_op jit(solution)/shard_map/reduce_scatter | solution.py:81
  204.7 1.7 copy-start.1
  228.4 49.1 %slice-start = ((s8[8388608]{0:T(1024)(128)(4,1)}), s8[4194304]{0:T(1024)(128)(4,1)S(1)}, s32[]{:S(2)}) async-start(s8[8388608]{0:T(1024)(128)(4,1)} %bitcast.56), calls=%async_computation.8 | async-start | bytes 8388608
  230.7 46.8 %slice-start.1 = ((s8[8388608]{0:T(1024)(128)(4,1)}), s8[4194304]{0:T(1024)(128)(4,1)S(1)}, s32[]{:S(2)}) async-start(s8[8388608]{0:T(1024)(128)(4,1)} %bitcast.56), calls=%async_computation.9 | async-start | bytes 8388608
  282.4 118.5 %reduce-scatter.3.cloned.1.call-start = ((), (), s32[]{:S(2)}) async-start(), calls=%async_computation.6 | async-start | bytes 3342336 | tf_op jit(solution)/shard_map/reduce_scatter | solution.py:81
  289.5 1.4 copy-start
Sparse Core Ops, SparseCore 0:
  10.4 78.7 all-gather.3
  91.1 45.7 all-gather.5
  282.6 56.6 reduce-scatter.4
  341.6 59.2 reduce-scatter.2
where the time goes:
time: 410 us; the launch traced here: 409 us
  waiting for transfers between devices  228 us (56%)
  blocking collectives  70.2 us (17%)
  local copies, waits for them, and re-layouts  48.4 us (12%)
  matrix products  24.9 us (6%)
  other arithmetic  16.6 us (4%)
  between operations  14 us (3%)
  starting transfers between devices  7.56 us (2%)
    reduce_scatter x2, waiting for transfers between devices, local(): lax.psum_scatter(part, 'dp', scatter_dimension=0, tiled=True)  105 us
    all_gather x1, waiting for transfers between devices, local(): cot_group = lax.all_gather(cotangent, 'expert', axis=0, tiled=True)  53.2 us
    all_to_all x1, blocking collectives, local(): lax.all_to_all(h_send, 'expert', split_axis=0, concat_axis=2, tiled=True)[0]  46.5 us
    all_to_all x1, waiting for transfers between devices, local(): lax.all_to_all(grads.reshape(1, local_experts, owners * capacity, hidden_...  41.3 us
    all_gather x1, waiting for transfers between devices, local(): full_down = lax.all_gather(w_down, 'dp', axis=1, tiled=True)  26.9 us
    all_gather x1, blocking collectives, local(): lax.all_gather(route_ids.reshape(1, routes), 'expert', axis=0, tiled=True)  23.6 us
    gather x1, local copies, waits for them, and re-layouts, local(): dy_recv = cot_group[rows]  20.8 us
    dot_general x2, matrix products, local(): jnp.einsum('sf,sd->fd', h_recv[j], dy_recv[j], preferred_element_type=jnp...  11.9 us
  transfers between devices with their start and end apart: 5, of which 5 were waited for; matrix products, arithmetic and copies ran while one was open for 10% of the time, Pallas kernels for 0%

commit v1 on v0

--- a/solution.py
+++ b/solution.py
@@ -25,7 +25,12 @@
     routes = tokens * top
     cot_group = lax.all_gather(cotangent, "expert", axis=0, tiled=True)
     ids_group = lax.all_gather(route_ids.reshape(1, routes), "expert", axis=0, tiled=True)
-    full_down = lax.all_gather(w_down, "dp", axis=1, tiled=True)
+    ring = [w_down]
+    for hop in range(15):
+        ring.append(lax.ppermute(ring[-1], "dp", [(dev, (dev + 1) % 16) for dev in range(16)]))
+    full_down = jnp.roll(
+        jnp.concatenate(ring[::-1], axis=1), (lax.axis_index("dp") + 1) * ring[0].shape[1], axis=1
+    )
     gate = saved_gate_up[:, :, :hidden_units].astype(jnp.float32)
     up = saved_gate_up[:, :, hidden_units:].astype(jnp.float32)
     sig = jax.nn.sigmoid(gate)

time: 410 us -> 476 us (1.16)
  local copies, waits for them, and re-layouts: 48.4 us -> 88.2 us
  waiting for transfers between devices: 228 us -> 259 us
  blocking collectives: 70.2 us -> 62.8 us
    ppermute x0 -> x15, waiting for transfers between devices: none -> 114 us  [local(): lax.ppermute(ring[-1], 'dp', [(dev, (dev + 1) % 16) for dev in range(16)])]
    all_gather x1, waiting for transfers between devices: 53.2 us -> 0.01 us  [local(): cot_group = lax.all_gather(cotangent, 'expert', axis=0, tiled=True)]
    unnamed x17 -> x62, local copies, waits for them, and re-layouts: 4.74 us -> 40.9 us
    all_gather x1 -> x0, waiting for transfers between devices: 26.9 us -> none  [local(): full_down = lax.all_gather(w_down, 'dp', axis=1, tiled=True)]
    all_to_all x1, waiting for transfers between devices: 41.3 us -> 31.8 us  [local(): lax.all_to_all(grads.reshape(1, local_experts, owners * capacity, hidden_...]
    reduce_scatter x2, waiting for transfers between devices: 105 us -> 112 us  [local(): lax.psum_scatter(part, 'dp', scatter_dimension=0, tiled=True)]
    all_to_all x1, blocking collectives: 46.5 us -> 39.1 us  [local(): lax.all_to_all(h_send, 'expert', split_axis=0, concat_axis=2, tiled=True)[0]]
  transfers between devices with their start and end apart: 5 -> 19, of which waited for: 5 -> 17; matrix products, arithmetic and copies ran while one was open for 10% -> 13% of each run, Pallas kernels for 0% -> 0%
where the time goes in v1:
time: 476 us; the launch traced here: 475 us
  waiting for transfers between devices  259 us (54%)
  local copies, waits for them, and re-layouts  88.2 us (19%)
  blocking collectives  62.8 us (13%)
  matrix products  27.4 us (6%)
  other arithmetic  18.8 us (4%)
  between operations  14 us (3%)
  starting transfers between devices  5.59 us (1%)
    ppermute x15, waiting for transfers between devices, local(): lax.ppermute(ring[-1], 'dp', [(dev, (dev + 1) % 16) for dev in range(16)])  114 us
    reduce_scatter x2, waiting for transfers between devices, local(): lax.psum_scatter(part, 'dp', scatter_dimension=0, tiled=True)  112 us
    unnamed x62, local copies, waits for them, and re-layouts  40.9 us
    all_to_all x1, blocking collectives, local(): lax.all_to_all(h_send, 'expert', split_axis=0, concat_axis=2, tiled=True)[0]  39.1 us
    all_to_all x1, waiting for transfers between devices, local(): lax.all_to_all(grads.reshape(1, local_experts, owners * capacity, hidden_...  31.8 us
    all_gather x1, blocking collectives, local(): lax.all_gather(route_ids.reshape(1, routes), 'expert', axis=0, tiled=True)  23.6 us
    gather x1, local copies, waits for them, and re-layouts, local(): dy_recv = cot_group[rows]  21 us
    dot_general x2, matrix products, local(): jnp.einsum('sf,sd->fd', h_recv[j], dy_recv[j], preferred_element_type=jnp...  12.8 us
  transfers between devices with their start and end apart: 19, of which 17 were waited for; matrix products, arithmetic and copies ran while one was open for 13% of the time, Pallas kernels for 0%

profile of v1, /device:TPU:2, one launch (start us, length us, event | category | flops | bytes accessed | tf_op | source)
XLA Modules:
  0.0 475.4 jit_solution(16396767701264473301)
XLA Ops:
  7.9 11.0 %collective-permute-done = bf16[2,48,2048]{2,1,0:T(8,128)(2,1)S(1)} collective-permute-done((bf16[2,48,2048]{2,1,0:T(8,128)(2,1)}, bf16[2,48,2048]{2,1,0:T(8,128)(2,1)S(1)}, u32[]{:S(2)}, u32[]{:S(2)}) %collective-permute-start) | collective-permute-done | bytes 393248 | tf_op jit(solution)/shard_map/ppermute | solution.py:30
  18.9 8.4 %collective-permute-done.1 = bf16[2,48,2048]{2,1,0:T(8,128)(2,1)S(1)} collective-permute-done((bf16[2,48,2048]{2,1,0:T(8,128)(2,1)S(1)}, bf16[2,48,2048]{2,1,0:T(8,128)(2,1)S(1)}, u32[]{:S(2)}, u32[]{:S(2)}) %collective-permute-start.1) | collective-permute-done | bytes 393248 | tf_op jit(solution)/shard_map/ppermute | solution.py:30
  27.3 8.4 %collective-permute-done.2 = bf16[2,48,2048]{2,1,0:T(8,128)(2,1)S(1)} collective-permute-done((bf16[2,48,2048]{2,1,0:T(8,128)(2,1)S(1)}, bf16[2,48,2048]{2,1,0:T(8,128)(2,1)S(1)}, u32[]{:S(2)}, u32[]{:S(2)}) %collective-permute-start.2) | collective-permute-done | bytes 393248 | tf_op jit(solution)/shard_map/ppermute | solution.py:30
  35.7 8.4 %collective-permute-done.3 = bf16[2,48,2048]{2,1,0:T(8,128)(2,1)S(1)} collective-permute-done((bf16[2,48,2048]{2,1,0:T(8,128)(2,1)S(1)}, bf16[2,48,2048]{2,1,0:T(8,128)(2,1)S(1)}, u32[]{:S(2)}, u32[]{:S(2)}) %collective-permute-start.3) | collective-permute-done | bytes 393248 | tf_op jit(solution)/shard_map/ppermute | solution.py:30
  44.1 8.4 %collective-permute-done.4 = bf16[2,48,2048]{2,1,0:T(8,128)(2,1)S(1)} collective-permute-done((bf16[2,48,2048]{2,1,0:T(8,128)(2,1)S(1)}, bf16[2,48,2048]{2,1,0:T(8,128)(2,1)S(1)}, u32[]{:S(2)}, u32[]{:S(2)}) %collective-permute-start.4) | collective-permute-done | bytes 393248 | tf_op jit(solution)/shard_map/ppermute | solution.py:30
  52.5 8.4 %collective-permute-done.5 = bf16[2,48,2048]{2,1,0:T(8,128)(2,1)S(1)} collective-permute-done((bf16[2,48,2048]{2,1,0:T(8,128)(2,1)S(1)}, bf16[2,48,2048]{2,1,0:T(8,128)(2,1)S(1)}, u32[]{:S(2)}, u32[]{:S(2)}) %collective-permute-start.5) | collective-permute-done | bytes 393248 | tf_op jit(solution)/shard_map/ppermute | solution.py:30
  61.0 8.4 %collective-permute-done.6 = bf16[2,48,2048]{2,1,0:T(8,128)(2,1)S(1)} collective-permute-done((bf16[2,48,2048]{2,1,0:T(8,128)(2,1)S(1)}, bf16[2,48,2048]{2,1,0:T(8,128)(2,1)S(1)}, u32[]{:S(2)}, u32[]{:S(2)}) %collective-permute-start.6) | collective-permute-done | bytes 393248 | tf_op jit(solution)/shard_map/ppermute | solution.py:30
  69.4 8.4 %collective-permute-done.7 = bf16[2,48,2048]{2,1,0:T(8,128)(2,1)S(1)} collective-permute-done((bf16[2,48,2048]{2,1,0:T(8,128)(2,1)S(1)}, bf16[2,48,2048]{2,1,0:T(8,128)(2,1)S(1)}, u32[]{:S(2)}, u32[]{:S(2)}) %collective-permute-start.7) | collective-permute-done | bytes 393248 | tf_op jit(solution)/shard_map/ppermute | solution.py:30
  77.8 8.4 %collective-permute-done.8 = bf16[2,48,2048]{2,1,0:T(8,128)(2,1)S(1)} collective-permute-done((bf16[2,48,2048]{2,1,0:T(8,128)(2,1)S(1)}, bf16[2,48,2048]{2,1,0:T(8,128)(2,1)S(1)}, u32[]{:S(2)}, u32[]{:S(2)}) %collective-permute-start.8) | collective-permute-done | bytes 393248 | tf_op jit(solution)/shard_map/ppermute | solution.py:30
  86.9 8.4 %collective-permute-done.9 = bf16[2,48,2048]{2,1,0:T(8,128)(2,1)S(1)} collective-permute-done((bf16[2,48,2048]{2,1,0:T(8,128)(2,1)S(1)}, bf16[2,48,2048]{2,1,0:T(8,128)(2,1)S(1)}, u32[]{:S(2)}, u32[]{:S(2)}) %collective-permute-start.9) | collective-permute-done | bytes 393248 | tf_op jit(solution)/shard_map/ppermute | solution.py:30
  95.4 1.4 copy.30
  97.7 23.6 %all-gather = s32[16,1,1024]{2,1,0:T(1,128)S(1)} all-gather(s32[1,1,1024]{2,1,0:T(1,128)S(1)} %reshape.205), channel_id=1, replica_groups=mesh['dp'=16,'expert'=16] {'expert'}, dimensions={0}, use_global_device_ids=true | all-gather | bytes 69632 | tf_op jit(solution)/shard_map/all_gather | solution.py:27
  122.6 2.9 fusion.31
  125.5 5.8 %collective-permute-done.11 = bf16[2,48,2048]{2,1,0:T(8,128)(2,1)} collective-permute-done((bf16[2,48,2048]{2,1,0:T(8,128)(2,1)}, bf16[2,48,2048]{2,1,0:T(8,128)(2,1)}, u32[]{:S(2)}, u32[]{:S(2)}) %collective-permute-start.11) | collective-permute-done | bytes 393248 | tf_op jit(solution)/shard_map/ppermute | solution.py:30
  132.4 7.7 %collective-permute-done.12 = bf16[2,48,2048]{2,1,0:T(8,128)(2,1)} collective-permute-done((bf16[2,48,2048]{2,1,0:T(8,128)(2,1)}, bf16[2,48,2048]{2,1,0:T(8,128)(2,1)}, u32[]{:S(2)}, u32[]{:S(2)}) %collective-permute-start.12) | collective-permute-done | bytes 393248 | tf_op jit(solution)/shard_map/ppermute | solution.py:30
  140.1 1.6 select_reduce_fusion.1
  143.2 5.6 %collective-permute-done.13 = bf16[2,48,2048]{2,1,0:T(8,128)(2,1)} collective-permute-done((bf16[2,48,2048]{2,1,0:T(8,128)(2,1)}, bf16[2,48,2048]{2,1,0:T(8,128)(2,1)}, u32[]{:S(2)}, u32[]{:S(2)}) %collective-permute-start.13) | collective-permute-done | bytes 393248 | tf_op jit(solution)/shard_map/ppermute | solution.py:30
  149.5 7.9 %collective-permute-done.14 = bf16[2,48,2048]{2,1,0:T(8,128)(2,1)S(1)} collective-permute-done((bf16[2,48,2048]{2,1,0:T(8,128)(2,1)}, bf16[2,48,2048]{2,1,0:T(8,128)(2,1)S(1)}, u32[]{:S(2)}, u32[]{:S(2)}) %collective-permute-start.14) | collective-permute-done | bytes 393248 | tf_op jit(solution)/shard_map/ppermute | solution.py:30
  158.2 1.8 constant_dynamic-update-slice_fusion.30
  160.0 1.8 constant_dynamic-update-slice_fusion.29
  161.8 1.8 constant_dynamic-update-slice_fusion.28
  163.6 1.8 constant_dynamic-update-slice_fusion.27
  165.4 1.8 constant_dynamic-update-slice_fusion.26
  167.1 1.7 constant_dynamic-update-slice_fusion.25
  176.7 1.8 constant_dynamic-update-slice_fusion.14
  178.5 1.8 constant_dynamic-update-slice_fusion.13
  180.2 1.8 constant_dynamic-update-slice_fusion.12
  182.0 1.8 constant_dynamic-update-slice_fusion.11
  192.4 21.0 %gather_fusion = bf16[2048,2048]{1,0:T(8,128)(2,1)} fusion(bf16[2048,2048]{1,0:T(8,128)(2,1)} %all-gather.3.cloned.1.call-done, s32[2048]{0:T(1024)S(1)} %bitcast_clamp_fusion), kind=kCustom, calls=%fused_computation | custom fusion | bytes 16785408 | tf_op jit(solution)/shard_map/gather | solution.py:68
  213.3 11.2 %convert_bitcast_fusion = bf16[1,2,1024,768]{3,2,1,0:T(8,128)(2,1)S(1)} fusion(bf16[2,1024,2048]{2,1,0:T(8,128)(2,1)} %bitcast.54, bf16[2,1536,2048]{2,1,0:T(8,128)(2,1)} %constant_dynamic-update-slice_fusion, s32[]{:T(128)S(6)} %select_n.69), kind=kOutput, calls=%fused_computation.40 | convolution fusion | flops 6444023808 | bytes 17825796 | tf_op jit(solution)/shard_map/jsd,jfd->jsf/dot_general | solution.py:70
  224.5 4.9 %copy.32 = bf16[1,2,1024,768]{3,1,0,2:T(2,128)(2,1)} copy(bf16[1,2,1024,768]{3,2,1,0:T(8,128)(2,1)S(1)} %convert_bitcast_fusion) | data formatting | bytes 6291456 | tf_op jit(solution)/shard_map/reshape | solution.py:74
  229.4 5.4 %all-to-all-start = ((bf16[1,2,1024,768]{3,1,0,2:T(2,128)(2,1)}), bf16[1,2,1024,768]{3,1,0,2:T(2,128)(2,1)S(1)}, u32[]{:S(2)}, u32[]{:S(2)}) async-start(bf16[1,2,1024,768]{3,1,0,2:T(2,128)(2,1)} %copy.32), calls=%async_computation | async-start | bytes 6291456 | tf_op jit(solution)/shard_map/all_to_all | solution.py:73
  235.9 1.0 fusion
  238.0 31.8 %all-to-all-done = bf16[1,2,1024,768]{3,1,0,2:T(2,128)(2,1)S(1)} async-done(((bf16[1,2,1024,768]{3,1,0,2:T(2,128)(2,1)}), bf16[1,2,1024,768]{3,1,0,2:T(2,128)(2,1)S(1)}, u32[]{:S(2)}, u32[]{:S(2)}) %all-to-all-start) | async-done | bytes 3145760 | tf_op jit(solution)/shard_map/all_to_all | solution.py:73
  269.8 1.7 copy-done.1
  271.5 2.5 copy.33
  274.0 5.4 %gather_fusion.1 = bf16[1024,768]{1,0:T(8,128)(2,1)} fusion(bf16[2048,768]{1,0:T(8,128)(2,1)S(1)} %bitcast.50, s32[1024]{0:T(1024)S(1)} %broadcast_clamp_fusion.1), kind=kCustom, calls=%fused_computation.1 | custom fusion | bytes 3149824 | tf_op jit(solution)/shard_map/gather | solution.py:89
  279.4 5.1 %fusion.33 = (bf16[1024,768]{1,0:T(8,128)(2,1)S(1)}, bf16[128,8,768]{2,1,0:T(8,128)(2,1)S(1)}, bf16[128,8,768]{2,1,0:T(8,128)(2,1)}, bf16[128,8,768]{2,1,0:T(8,128)(2,1)}) fusion(f32[128,8]{1,0:T(8,128)S(1)} %copy.29, bf16[128,8,1536]{2,1,0:T(8,128)(2,1)} %param.6, bf16[1024,768]{1,0:T(8,128)(2,1)} %gather_fusion.1), kind=kLoop, calls=%fused_computation.46 | loop fusion | flops 17301504 | bytes 11014144 | tf_op jit(solution)/shard_map/reshape | solution.py:52
  284.5 9.4 %gather_fusion.2 = bf16[2048,768]{1,0:T(8,128)(2,1)} fusion(bf16[1024,768]{1,0:T(8,128)(2,1)S(1)} %get-tuple-element.9, s32[2048]{0:T(1024)S(1)} %broadcast_clamp_fusion), kind=kCustom, calls=%fused_computation.2 | custom fusion | bytes 6299648 | tf_op jit(solution)/shard_map/gather | solution.py:52
  293.9 2.3 broadcast_select_fusion
  296.2 39.1 %all_to_all.30 = bf16[16,2,64,768]{3,2,1,0:T(8,128)(2,1)S(1)} all-to-all(bf16[16,2,64,768]{3,2,1,0:T(8,128)(2,1)S(1)} %broadcast_select_fusion), channel_id=1, replica_groups=mesh['dp'=16,'expert'=16] {'expert'}, dimensions={0} | all-to-all | bytes 6291456 | tf_op jit(solution)/shard_map/all_to_all | solution.py:69
  335.3 1.4 fusion.47
  336.7 4.9 %fusion.12 = bf16[768,2048]{1,0:T(8,128)(2,1)} fusion(bf16[1024,768]{1,0:T(8,128)(2,1)S(1)} %bitcast.58, bf16[2048,2048]{1,0:T(8,128)(2,1)S(1)} %bitcast.56), kind=kOutput, calls=%fused_computation.26 | convolution fusion | flops 3222798336 | bytes 8912896 | tf_op jit(solution)/shard_map/sf,sd->fd/dot_general | solution.py:82
  341.6 7.9 %fusion.15 = bf16[768,2048]{1,0:T(8,128)(2,1)} fusion(bf16[1024,768]{1,0:T(8,128)(2,1)} %bitcast.57, bf16[2048,2048]{1,0:T(8,128)(2,1)} %gather_fusion), kind=kOutput, calls=%fused_computation.27 | convolution fusion | flops 3222798336 | bytes 8912896 | tf_op jit(solution)/shard_map/sf,sd->fd/dot_general | solution.py:82
  350.7 3.8 pad_maximum_fusion
  354.5 50.4 %reduce-scatter.3.cloned.1.call-done = bf16[48,2048]{1,0:T(8,128)(2,1)} async-done(((bf16[768,2048]{1,0:T(8,128)(2,1)}), bf16[48,2048]{1,0:T(8,128)(2,1)}) %reduce-scatter.3.cloned.1.call-update) | async-done | bytes 196624 | tf_op jit(solution)/shard_map/reduce_scatter | solution.py:86
  404.9 62.1 %reduce-scatter.5.cloned.1.call-done = bf16[48,2048]{1,0:T(8,128)(2,1)} async-done(((bf16[768,2048]{1,0:T(8,128)(2,1)}), bf16[48,2048]{1,0:T(8,128)(2,1)}) %reduce-scatter.5.cloned.1.call-update) | async-done | bytes 196624 | tf_op jit(solution)/shard_map/reduce_scatter | solution.py:86
  467.0 2.0 maximum_convert_fusion
  (101 shorter events, 27.5 us)
Async XLA Ops:
  7.2 185.2 %all-gather.3.cloned.1.call-start = ((), (), s32[]{:S(2)}) async-start(), calls=%async_computation.4 | async-start | bytes 8912896 | tf_op jit(solution)/shard_map/all_gather | solution.py:26
  7.9 11.0 %collective-permute-start = (bf16[2,48,2048]{2,1,0:T(8,128)(2,1)}, bf16[2,48,2048]{2,1,0:T(8,128)(2,1)S(1)}, u32[]{:S(2)}, u32[]{:S(2)}) collective-permute-start(bf16[2,48,2048]{2,1,0:T(8,128)(2,1)} %param.9), channel_id=1, source_target_pairs={{0,16},{16,32},{32,48},{48,64},{64,80},{80,96},{96,112},{112,128},... | collective-permute-start | bytes 1179656 | tf_op jit(solution)/shard_map/ppermute | solution.py:30
  18.9 8.4 %collective-permute-start.1 = (bf16[2,48,2048]{2,1,0:T(8,128)(2,1)S(1)}, bf16[2,48,2048]{2,1,0:T(8,128)(2,1)S(1)}, u32[]{:S(2)}, u32[]{:S(2)}) collective-permute-start(bf16[2,48,2048]{2,1,0:T(8,128)(2,1)S(1)} %collective-permute-done), channel_id=1, source_target_pairs={{0,16},{16,32},{32,48},{48,64},{64,80},{80,96},{96,112},{112,128},... | collective-permute-start | bytes 1179656 | tf_op jit(solution)/shard_map/ppermute | solution.py:30
  27.3 8.4 %collective-permute-start.2 = (bf16[2,48,2048]{2,1,0:T(8,128)(2,1)S(1)}, bf16[2,48,2048]{2,1,0:T(8,128)(2,1)S(1)}, u32[]{:S(2)}, u32[]{:S(2)}) collective-permute-start(bf16[2,48,2048]{2,1,0:T(8,128)(2,1)S(1)} %collective-permute-done.1), channel_id=1, source_target_pairs={{0,16},{16,32},{32,48},{48,64},{64,80},{80,96},{96,112},{112,128},... | collective-permute-start | bytes 1179656 | tf_op jit(solution)/shard_map/ppermute | solution.py:30
  35.7 8.4 %collective-permute-start.3 = (bf16[2,48,2048]{2,1,0:T(8,128)(2,1)S(1)}, bf16[2,48,2048]{2,1,0:T(8,128)(2,1)S(1)}, u32[]{:S(2)}, u32[]{:S(2)}) collective-permute-start(bf16[2,48,2048]{2,1,0:T(8,128)(2,1)S(1)} %collective-permute-done.2), channel_id=1, source_target_pairs={{0,16},{16,32},{32,48},{48,64},{64,80},{80,96},{96,112},{112,128},... | collective-permute-start | bytes 1179656 | tf_op jit(solution)/shard_map/ppermute | solution.py:30
  44.1 8.4 %collective-permute-start.4 = (bf16[2,48,2048]{2,1,0:T(8,128)(2,1)S(1)}, bf16[2,48,2048]{2,1,0:T(8,128)(2,1)S(1)}, u32[]{:S(2)}, u32[]{:S(2)}) collective-permute-start(bf16[2,48,2048]{2,1,0:T(8,128)(2,1)S(1)} %collective-permute-done.3), channel_id=1, source_target_pairs={{0,16},{16,32},{32,48},{48,64},{64,80},{80,96},{96,112},{112,128},... | collective-permute-start | bytes 1179656 | tf_op jit(solution)/shard_map/ppermute | solution.py:30
  52.5 8.4 %collective-permute-start.5 = (bf16[2,48,2048]{2,1,0:T(8,128)(2,1)S(1)}, bf16[2,48,2048]{2,1,0:T(8,128)(2,1)S(1)}, u32[]{:S(2)}, u32[]{:S(2)}) collective-permute-start(bf16[2,48,2048]{2,1,0:T(8,128)(2,1)S(1)} %collective-permute-done.4), channel_id=1, source_target_pairs={{0,16},{16,32},{32,48},{48,64},{64,80},{80,96},{96,112},{112,128},... | collective-permute-start | bytes 1179656 | tf_op jit(solution)/shard_map/ppermute | solution.py:30
  60.9 8.4 %collective-permute-start.6 = (bf16[2,48,2048]{2,1,0:T(8,128)(2,1)S(1)}, bf16[2,48,2048]{2,1,0:T(8,128)(2,1)S(1)}, u32[]{:S(2)}, u32[]{:S(2)}) collective-permute-start(bf16[2,48,2048]{2,1,0:T(8,128)(2,1)S(1)} %collective-permute-done.5), channel_id=1, source_target_pairs={{0,16},{16,32},{32,48},{48,64},{64,80},{80,96},{96,112},{112,128},... | collective-permute-start | bytes 1179656 | tf_op jit(solution)/shard_map/ppermute | solution.py:30
  69.4 8.4 %collective-permute-start.7 = (bf16[2,48,2048]{2,1,0:T(8,128)(2,1)S(1)}, bf16[2,48,2048]{2,1,0:T(8,128)(2,1)S(1)}, u32[]{:S(2)}, u32[]{:S(2)}) collective-permute-start(bf16[2,48,2048]{2,1,0:T(8,128)(2,1)S(1)} %collective-permute-done.6), channel_id=1, source_target_pairs={{0,16},{16,32},{32,48},{48,64},{64,80},{80,96},{96,112},{112,128},... | collective-permute-start | bytes 1179656 | tf_op jit(solution)/shard_map/ppermute | solution.py:30
  77.8 8.4 %collective-permute-start.8 = (bf16[2,48,2048]{2,1,0:T(8,128)(2,1)S(1)}, bf16[2,48,2048]{2,1,0:T(8,128)(2,1)S(1)}, u32[]{:S(2)}, u32[]{:S(2)}) collective-permute-start(bf16[2,48,2048]{2,1,0:T(8,128)(2,1)S(1)} %collective-permute-done.7), channel_id=1, source_target_pairs={{0,16},{16,32},{32,48},{48,64},{64,80},{80,96},{96,112},{112,128},... | collective-permute-start | bytes 1179656 | tf_op jit(solution)/shard_map/ppermute | solution.py:30
  86.2 0.7 copy-start.3
  86.9 8.4 %collective-permute-start.9 = (bf16[2,48,2048]{2,1,0:T(8,128)(2,1)S(1)}, bf16[2,48,2048]{2,1,0:T(8,128)(2,1)S(1)}, u32[]{:S(2)}, u32[]{:S(2)}) collective-permute-start(bf16[2,48,2048]{2,1,0:T(8,128)(2,1)S(1)} %collective-permute-done.8), channel_id=1, source_target_pairs={{0,16},{16,32},{32,48},{48,64},{64,80},{80,96},{96,112},{112,128},... | collective-permute-start | bytes 1179656 | tf_op jit(solution)/shard_map/ppermute | solution.py:30
  95.3 27.3 %copy-start.5 = (bf16[2,48,2048]{2,1,0:T(8,128)(2,1)}, bf16[2,48,2048]{2,1,0:T(8,128)(2,1)S(1)}, u32[]{:S(2)}) copy-start(bf16[2,48,2048]{2,1,0:T(8,128)(2,1)S(1)} %collective-permute-done.9) | copy-start | bytes 1179652
  95.3 27.3 %collective-permute-start.10 = (bf16[2,48,2048]{2,1,0:T(8,128)(2,1)S(1)}, bf16[2,48,2048]{2,1,0:T(8,128)(2,1)}, u32[]{:S(2)}, u32[]{:S(2)}) collective-permute-start(bf16[2,48,2048]{2,1,0:T(8,128)(2,1)S(1)} %collective-permute-done.9), channel_id=1, source_target_pairs={{0,16},{16,32},{32,48},{48,64},{64,80},{80,96},{96,112},{112,128},... | collective-permute-start | bytes 1179656 | tf_op jit(solution)/shard_map/ppermute | solution.py:30
  121.4 0.6 copy-start.7
  122.6 8.7 %collective-permute-start.11 = (bf16[2,48,2048]{2,1,0:T(8,128)(2,1)}, bf16[2,48,2048]{2,1,0:T(8,128)(2,1)}, u32[]{:S(2)}, u32[]{:S(2)}) collective-permute-start(bf16[2,48,2048]{2,1,0:T(8,128)(2,1)} %collective-permute-done.10), channel_id=1, source_target_pairs={{0,16},{16,32},{32,48},{48,64},{64,80},{80,96},{96,112},{112,128},... | collective-permute-start | bytes 1179656 | tf_op jit(solution)/shard_map/ppermute | solution.py:30
  122.6 52.5 %copy-start.2 = (bf16[2,48,2048]{2,1,0:T(8,128)(2,1)S(1)}, bf16[2,48,2048]{2,1,0:T(8,128)(2,1)}, u32[]{:S(2)}) copy-start(bf16[2,48,2048]{2,1,0:T(8,128)(2,1)} %param.9) | copy-start | bytes 1179652
  131.3 8.7 %collective-permute-start.12 = (bf16[2,48,2048]{2,1,0:T(8,128)(2,1)}, bf16[2,48,2048]{2,1,0:T(8,128)(2,1)}, u32[]{:S(2)}, u32[]{:S(2)}) collective-permute-start(bf16[2,48,2048]{2,1,0:T(8,128)(2,1)} %collective-permute-done.11), channel_id=1, source_target_pairs={{0,16},{16,32},{32,48},{48,64},{64,80},{80,96},{96,112},{112,128},... | collective-permute-start | bytes 1179656 | tf_op jit(solution)/shard_map/ppermute | solution.py:30
  140.1 8.7 %collective-permute-start.13 = (bf16[2,48,2048]{2,1,0:T(8,128)(2,1)}, bf16[2,48,2048]{2,1,0:T(8,128)(2,1)}, u32[]{:S(2)}, u32[]{:S(2)}) collective-permute-start(bf16[2,48,2048]{2,1,0:T(8,128)(2,1)} %collective-permute-done.12), channel_id=1, source_target_pairs={{0,16},{16,32},{32,48},{48,64},{64,80},{80,96},{96,112},{112,128},... | collective-permute-start | bytes 1179656 | tf_op jit(solution)/shard_map/ppermute | solution.py:30
  143.2 40.6 %copy-start.6 = (bf16[2,48,2048]{2,1,0:T(8,128)(2,1)S(1)}, bf16[2,48,2048]{2,1,0:T(8,128)(2,1)}, u32[]{:S(2)}) copy-start(bf16[2,48,2048]{2,1,0:T(8,128)(2,1)} %copy-done.5) | copy-start | bytes 1179652
  148.8 8.6 %collective-permute-start.14 = (bf16[2,48,2048]{2,1,0:T(8,128)(2,1)}, bf16[2,48,2048]{2,1,0:T(8,128)(2,1)S(1)}, u32[]{:S(2)}, u32[]{:S(2)}) collective-permute-start(bf16[2,48,2048]{2,1,0:T(8,128)(2,1)} %collective-permute-done.13), channel_id=1, source_target_pairs={{0,16},{16,32},{32,48},{48,64},{64,80},{80,96},{96,112},{112,128},... | collective-permute-start | bytes 1179656 | tf_op jit(solution)/shard_map/ppermute | solution.py:30
  158.2 26.4 %copy-start.4 = (bf16[2,48,2048]{2,1,0:T(8,128)(2,1)S(1)}, bf16[2,48,2048]{2,1,0:T(8,128)(2,1)}, u32[]{:S(2)}) copy-start(bf16[2,48,2048]{2,1,0:T(8,128)(2,1)} %copy-done.3) | copy-start | bytes 1179652
  224.5 10.4 %copy-start.8 = (s32[128,8]{1,0:T(8,128)S(1)}, s32[128,8]{1,0:T(8,128)}, u32[]{:S(2)}) copy-start(s32[128,8]{1,0:T(8,128)} %copy.30) | copy-start | bytes 12292
  224.5 11.1 %copy-start.9 = (s32[128,8]{0,1:T(8,128)S(1)}, s32[128,8]{0,1:T(8,128)}, u32[]{:S(2)}) copy-start(s32[128,8]{0,1:T(8,128)} %param.7) | copy-start | bytes 12292
  224.5 11.3 %copy-start.10 = (f32[128,8]{0,1:T(8,128)S(1)}, f32[128,8]{0,1:T(8,128)}, u32[]{:S(2)}) copy-start(f32[128,8]{0,1:T(8,128)} %param.8) | copy-start | bytes 12292
  229.4 40.4 %all-to-all-start = ((bf16[1,2,1024,768]{3,1,0,2:T(2,128)(2,1)}), bf16[1,2,1024,768]{3,1,0,2:T(2,128)(2,1)S(1)}, u32[]{:S(2)}, u32[]{:S(2)}) async-start(bf16[1,2,1024,768]{3,1,0,2:T(2,128)(2,1)} %copy.32), calls=%async_computation | async-start | bytes 6291456 | tf_op jit(solution)/shard_map/all_to_all | solution.py:73
  234.8 170.0 %reduce-scatter.3.cloned.1.call-start = ((), (), s32[]{:S(2)}) async-start(), calls=%async_computation.5 | async-start | bytes 3342336 | tf_op jit(solution)/shard_map/reduce_scatter | solution.py:86
  269.8 1.7 copy-start.1
  293.9 42.8 %slice-start = ((s8[8388608]{0:T(1024)(128)(4,1)}), s8[4194304]{0:T(1024)(128)(4,1)S(1)}, s32[]{:S(2)}) async-start(s8[8388608]{0:T(1024)(128)(4,1)} %bitcast.55), calls=%async_computation.7 | async-start | bytes 8388608
  296.1 40.5 %slice-start.1 = ((s8[8388608]{0:T(1024)(128)(4,1)}), s8[4194304]{0:T(1024)(128)(4,1)S(1)}, s32[]{:S(2)}) async-start(s8[8388608]{0:T(1024)(128)(4,1)} %bitcast.55), calls=%async_computation.8 | async-start | bytes 8388608
  341.5 8.0 %copy-start = (bf16[1024,768]{1,0:T(8,128)(2,1)S(1)}, bf16[1024,768]{1,0:T(8,128)(2,1)}, u32[]{:S(2)}) copy-start(bf16[1024,768]{1,0:T(8,128)(2,1)} %gather_fusion.1) | copy-start | bytes 4718596
  341.6 125.4 %reduce-scatter.5.cloned.1.call-start = ((), (), s32[]{:S(2)}) async-start(), calls=%async_computation.6 | async-start | bytes 3342336 | tf_op jit(solution)/shard_map/reduce_scatter | solution.py:86
Sparse Core Ops, SparseCore 0:
  10.4 78.6 all-gather.2
  341.7 63.1 reduce-scatter.2
  407.4 59.4 reduce-scatter.4
